TPU v7x, 512 devices: a whole 4x4x16 slice. The times are simulated.
512 devices in a mesh: row: 32 (over z, core), col: 16 (over x, y).
Axes of the slice: x: 4, y: 4, z: 16, core: 2. Of those that a mesh axis runs over, the one named last changes fastest.
Arguments:
- trailing: float32 [16384, 16384], P('row', 'col'), may hold values from -6 to 6
- panel: float32 [16384, 512], P(('row', 'col')), may hold values from -0.25 to 0.25
- inv_factor: float32 [512, 512], P(None, 'col'), as said below
- later_series: float32 [16384, 1024], P('row', 'col'), may hold values from -6 to 6
- fold_series: float32 [512, 1024], P('row', 'col'), may hold values from -6 to 6
- fold_len: int32 [1024], P('col'), may hold values from 1 to 32, as said below
Outputs:
- new_trailing: float32 [16384, 16384], P('row', 'col')
- new_series: float32 [16384, 1024], P('row', 'col')
Inputs may be any that keep to these rules, and one draw needn't show every extreme that they name: inv_factor is lower triangular with a diagonal between 1 and 2. `fold_len`: some series reach all 32 blocks and some only one.
All inputs are finite; a program needn't handle non-finite values.
Results may differ from a plain program's by a relative error of at most 0.0003.
Values sent between devices are 32-bit elements; how exact they have to be, the bound alone decides.
No kernel may reach another device: no remote copies, remote signals or barrier semaphores. Data moves between devices by JAX's collectives and lax.ppermute only.
A program may use at most 64 MiB of HBM per device.

v0:
```python
import jax
import jax.numpy as jnp
from jax import lax
from jax.sharding import PartitionSpec as P


def spread(array, axis, root):
    mine = lax.axis_index(axis) == root
    return lax.psum(jnp.where(mine, array, jnp.zeros_like(array)), axis)


def on_device(trailing, panel, inv_factor, later_series, fold_series, fold_len):
    highest = lax.Precision.HIGHEST
    contract = (((1,), (1,)), ((), ()))
    inverse = lax.all_gather(inv_factor, "col", axis=1, tiled=True)
    solved_mine = lax.dot_general(
        panel, inverse, contract, precision=highest, preferred_element_type=jnp.float32
    )
    row_block = lax.all_gather(solved_mine, "col", axis=0, tiled=True)
    rows_here = trailing.shape[0]
    cols_here = trailing.shape[1]
    tiles_across = cols_here // rows_here
    row_pos = lax.axis_index("row")
    col_pos = lax.axis_index("col")
    pieces = []
    for offset in range(tiles_across):
        source = col_pos * tiles_across + offset
        pieces.append(spread(row_block, "row", source))
    col_panel = jnp.concatenate(pieces, 0)
    update = lax.dot_general(
        row_block, col_panel, contract, precision=highest, preferred_element_type=jnp.float32
    )
    col_tile = (col_pos * cols_here + jnp.arange(cols_here, dtype=jnp.int32)) // rows_here
    lower = col_tile <= row_pos
    new_trailing = jnp.where(lower[None, :], trailing - update, trailing)
    fold_all = lax.all_gather(fold_series, "row", axis=0, tiled=True)
    innovations = jnp.dot(inverse, fold_all, precision=highest, preferred_element_type=jnp.float32)
    correction = jnp.dot(
        row_block, innovations, precision=highest, preferred_element_type=jnp.float32
    )
    active = row_pos < fold_len
    new_series = jnp.where(active[None, :], later_series - correction, later_series)
    return (new_trailing, new_series)


def solution(mesh):
    in_specs = (
        P("row", "col"),
        P(("row", "col"), None),
        P(None, "col"),
        P("row", "col"),
        P("row", "col"),
        P("col"),
    )
    out_specs = (P("row", "col"), P("row", "col"))
    return jax.shard_map(
        on_device, mesh=mesh, in_specs=in_specs, out_specs=out_specs, check_vma=False
    )
```

profile of v0, /device:TPU:1, one launch (start us, length us, event | category | flops | bytes accessed | tf_op | source)
XLA Modules:
  0.0 367.0 jit_solution(11055402713785752273)
XLA Ops:
  7.2 0.0 copy-start
  7.2 0.0 all-gather.3.cloned.1.call-start
  7.2 0.7 all-gather.3.cloned.1.call-update
  7.9 0.0 all-gather.5.cloned.1.call-start
  8.0 64.4 %all-gather.3.cloned.1.call-done = f32[512,512]{0,1:T(8,128)} async-done(((f32[512,32]{0,1:T(8,128)}), f32[512,512]{0,1:T(8,128)}) %all-gather.3.cloned.1.call-update) | async-done | bytes 1048592 | tf_op jit(solution)/shard_map/all_gather | solution.py:15
  72.3 0.0 copy-done
  72.3 2.6 fusion.12
  74.9 0.0 all-gather.5.cloned.1.call-update
  74.9 0.0 all-reduce.3.cloned.1.call-start
  75.0 0.0 copy-start.4
  75.0 0.0 copy-start.5
  75.0 0.0 copy-start.2
  75.0 58.2 %all-gather.5.cloned.1.call-done = f32[512,512]{1,0:T(8,128)} async-done(((f32[32,512]{1,0:T(8,128)}), f32[512,512]{1,0:T(8,128)}) %all-gather.5.cloned.1.call-update) | async-done | bytes 1048592 | tf_op jit(solution)/shard_map/all_gather | solution.py:19
  133.2 2.8 broadcast_select_fusion.1
  136.0 0.0 copy-start.1
  136.0 0.0 copy-start.3
  136.0 0.0 all-reduce.3.cloned.1.call-update
  136.1 0.0 copy-done.4
  136.1 34.2 %all_gather.11 = f32[512,64]{1,0:T(8,128)S(1)} all-gather(f32[16,64]{1,0:T(8,128)S(1)} %copy-done.4), channel_id=1, replica_groups=mesh['row'=32,'col'=16] {'row'}, dimensions={0}, use_global_device_ids=true | all-gather | bytes 135168 | tf_op jit(solution)/shard_map/all_gather | solution.py:36
  170.3 0.0 copy-done.5
  170.3 0.0 copy-done.2
  170.3 1.8 fusion.13
  172.1 0.0 copy-done.1
  172.1 0.0 copy-done.3
  172.1 1.8 fusion.6
  174.0 179.8 %all-reduce.3.cloned.1.call-done = (f32[512,512]{1,0:T(8,128)}, f32[512,512]{1,0:T(8,128)}) async-done(((f32[512,512]{1,0:T(8,128)}, f32[512,512]{1,0:T(8,128)}), (f32[512,512]{1,0:T(8,128)}, f32[512,512]{1,0:T(8,128)})) %all-reduce.3.cloned.1.call-update) | async-done | bytes 2097168 | tf_op jit(solution)/shard_map/psum | solution.py:9
  353.7 6.7 %subtract_select_fusion = f32[512,1024]{1,0:T(8,128)} fusion(f32[512,1024]{1,0:T(8,128)} %param.6, f32[512,512]{1,0:T(8,128)S(1)} %copy-done.1, f32[512,512]{1,0:T(8,128)} %get-tuple-element.2, f32[512,512]{1,0:T(8,128)} %get-tuple-element.3, pred[1024]{0:T(1024)(128)(4,1)S(1)} %fusion.8), kind=kOutput, calls=%fused_computation | convolution fusion | flops 3222798336 | bytes 7341056 | tf_op jit(solution)/shard_map/dot_general | solution.py:30
  (2 shorter events, 0.0 us)
Async XLA Ops:
  7.2 65.2 %copy-start = (f32[32,512]{1,0:T(8,128)S(1)}, f32[32,512]{1,0:T(8,128)}, u32[]{:S(2)}) copy-start(f32[32,512]{1,0:T(8,128)} %param.7) | copy-start | bytes 196612
  7.2 65.1 %all-gather.3.cloned.1.call-start = ((), (), s32[]{:S(2)}) async-start(), calls=%async_computation | async-start | bytes 1114112 | tf_op jit(solution)/shard_map/all_gather | solution.py:15
  7.9 125.3 %all-gather.5.cloned.1.call-start = ((), (), s32[]{:S(2)}) async-start(), calls=%async_computation.1 | async-start | bytes 1114112 | tf_op jit(solution)/shard_map/all_gather | solution.py:19
  74.9 278.8 %all-reduce.3.cloned.1.call-start = ((), (), s32[]{:S(2)}) async-start(), calls=%async_computation.2 | async-start | bytes 4194304 | tf_op jit(solution)/shard_map/psum | solution.py:9
  75.0 61.1 %copy-start.4 = (f32[16,64]{1,0:T(8,128)S(1)}, f32[16,64]{1,0:T(8,128)}, u32[]{:S(2)}) copy-start(f32[16,64]{1,0:T(8,128)} %param.10) | copy-start | bytes 12292
  75.0 95.3 %copy-start.5 = (s32[64]{0:T(128)S(1)}, s32[64]{0:T(128)}, u32[]{:S(2)}) copy-start(s32[64]{0:T(128)} %param.11) | copy-start | bytes 772
  75.0 95.3 %copy-start.2 = (f32[512,512]{0,1:T(8,128)S(1)}, f32[512,512]{0,1:T(8,128)}, u32[]{:S(2)}) copy-start(f32[512,512]{0,1:T(8,128)} %all-gather.3.cloned.1.call-done) | copy-start | bytes 3145732
  136.0 36.1 %copy-start.1 = (f32[512,512]{1,0:T(8,128)S(1)}, f32[512,512]{1,0:T(8,128)}, u32[]{:S(2)}) copy-start(f32[512,512]{1,0:T(8,128)} %all-gather.5.cloned.1.call-done) | copy-start | bytes 3145732
  136.0 36.1 %copy-start.3 = (f32[512,64]{0,1:T(8,128)S(1)}, f32[512,64]{0,1:T(8,128)}, u32[]{:S(2)}) copy-start(f32[512,64]{0,1:T(8,128)} %param.9) | copy-start | bytes 393220
Sparse Core Ops, SparseCore 0:
  11.0 61.2 all-gather.2
  75.9 57.2 all-gather.4
  136.2 217.5 all-reduce.2
where the time goes:
time: 367 us
  waiting for transfers between devices  303 us (83%)
  blocking collectives  34.2 us (9%)
  between operations  13.8 us (4%)
  matrix products  12.9 us (4%)
    psum x1, waiting for transfers between devices, spread(): return lax.psum(jnp.where(mine, array, jnp.zeros_like(array)), axis)  180 us
    all_gather x1, waiting for transfers between devices, on_device(): inverse = lax.all_gather(inv_factor, 'col', axis=1, tiled=True)  64.4 us
    all_gather x1, waiting for transfers between devices, on_device(): row_block = lax.all_gather(solved_mine, 'col', axis=0, tiled=True)  58.2 us
    all_gather x1, blocking collectives, on_device(): fold_all = lax.all_gather(fold_series, 'row', axis=0, tiled=True)  34.2 us
  transfers between devices with their start and end apart: 3, of which 3 were waited for; matrix products, arithmetic and copies ran while one was open for 1% of the time, Pallas kernels for 0%

commit v1 on v0

--- a/solution.py
+++ b/solution.py
@@ -16,7 +16,9 @@
     solved_mine = lax.dot_general(
         panel, inverse, contract, precision=highest, preferred_element_type=jnp.float32
     )
-    row_block = lax.all_gather(solved_mine, "col", axis=0, tiled=True)
+    row_block = jnp.concatenate(
+        lax.all_to_all(jnp.stack([solved_mine] * lax.axis_size("col")), "col", 0, 0), axis=0
+    )
     rows_here = trailing.shape[0]
     cols_here = trailing.shape[1]
     tiles_across = cols_here // rows_here

time: 367 us -> 327 us (0.89)
  waiting for transfers between devices: 303 us -> 258 us
  starting transfers between devices: 0.12 us -> 4.45 us
    all_gather x1 -> x0, waiting for transfers between devices: 58.2 us -> none  [on_device(): row_block = lax.all_gather(solved_mine, 'col', axis=0, tiled=True)]
    all_to_all x0 -> x1, waiting for transfers between devices: none -> 14.2 us  [on_device(): lax.all_to_all(jnp.stack([solved_mine] * lax.axis_size('col')), 'col', 0, 0)]
    all_to_all x0 -> x1, starting transfers between devices: none -> 4.37 us  [on_device(): lax.all_to_all(jnp.stack([solved_mine] * lax.axis_size('col')), 'col', 0, 0)]
where the time goes in v1:
time: 327 us
  waiting for transfers between devices  258 us (79%)
  blocking collectives  35.5 us (11%)
  between operations  14.1 us (4%)
  matrix products  12.2 us (4%)
  starting transfers between devices  4.45 us (1%)
    psum x1, waiting for transfers between devices, spread(): return lax.psum(jnp.where(mine, array, jnp.zeros_like(array)), axis)  179 us
    all_gather x1, waiting for transfers between devices, on_device(): inverse = lax.all_gather(inv_factor, 'col', axis=1, tiled=True)  64.4 us
    all_gather x1, blocking collectives, on_device(): fold_all = lax.all_gather(fold_series, 'row', axis=0, tiled=True)  35.5 us
    all_to_all x1, waiting for transfers between devices, on_device(): lax.all_to_all(jnp.stack([solved_mine] * lax.axis_size('col')), 'col', 0, 0)  14.2 us
    dot_general x1, matrix products, on_device(): lax.dot_general(row_block, col_panel, contract, precision=highest, prefer...  6.69 us
  transfers between devices with their start and end apart: 3, of which 3 were waited for; matrix products, arithmetic and copies ran while one was open for 1% of the time, Pallas kernels for 0%

profile of v1, /device:TPU:1, one launch (start us, length us, event | category | flops | bytes accessed | tf_op | source)
XLA Modules:
  0.0 327.0 jit_solution(6694178178313173914)
XLA Ops:
  7.2 0.0 copy-start
  7.2 0.0 all-gather.2.cloned.1.call-start
  7.2 0.7 all-gather.2.cloned.1.call-update
  7.9 64.4 %all-gather.2.cloned.1.call-done = f32[512,512]{0,1:T(8,128)} async-done(((f32[512,32]{0,1:T(8,128)}), f32[512,512]{0,1:T(8,128)}) %all-gather.2.cloned.1.call-update) | async-done | bytes 1048592 | tf_op jit(solution)/shard_map/all_gather | solution.py:15
  72.3 0.0 copy-done
  72.3 1.9 fusion.12
  74.3 1.1 stack.2
  75.4 4.4 %all-to-all-start = ((f32[16,32,512]{2,1,0:T(8,128)}), f32[16,32,512]{2,1,0:T(8,128)S(1)}, u32[]{:S(2)}, u32[]{:S(2)}) async-start(f32[16,32,512]{2,1,0:T(8,128)} %stack.2), calls=%async_computation | async-start | bytes 2097152 | tf_op jit(solution)/shard_map/all_to_all | solution.py:20
  79.7 0.0 all-reduce.3.cloned.1.call-start
  79.8 0.0 copy-start.3
  79.8 0.0 copy-start.4
  79.8 0.0 copy-start.1
  79.8 14.2 %all-to-all-done = f32[16,32,512]{2,1,0:T(8,128)S(1)} async-done(((f32[16,32,512]{2,1,0:T(8,128)}), f32[16,32,512]{2,1,0:T(8,128)S(1)}, u32[]{:S(2)}, u32[]{:S(2)}) %all-to-all-start) | async-done | bytes 1048608 | tf_op jit(solution)/shard_map/all_to_all | solution.py:20
  94.0 1.6 broadcast_select_fusion.1
  95.6 0.0 copy-start.2
  95.6 0.0 all-reduce.3.cloned.1.call-update
  95.6 0.0 copy-done.3
  95.6 35.5 %all_gather.7 = f32[512,64]{1,0:T(8,128)S(1)} all-gather(f32[16,64]{1,0:T(8,128)S(1)} %copy-done.3), channel_id=1, replica_groups=mesh['row'=32,'col'=16] {'row'}, dimensions={0}, use_global_device_ids=true | all-gather | bytes 135168 | tf_op jit(solution)/shard_map/all_gather | solution.py:38
  131.2 0.0 copy-done.4
  131.2 0.0 copy-done.1
  131.2 1.8 fusion.13
  133.0 0.0 copy-done.2
  133.0 1.8 fusion.6
  134.8 178.6 %all-reduce.3.cloned.1.call-done = (f32[512,512]{1,0:T(8,128)}, f32[512,512]{1,0:T(8,128)}) async-done(((f32[512,512]{1,0:T(8,128)}, f32[512,512]{1,0:T(8,128)}), (f32[512,512]{1,0:T(8,128)}, f32[512,512]{1,0:T(8,128)})) %all-reduce.3.cloned.1.call-update) | async-done | bytes 2097168 | tf_op jit(solution)/shard_map/psum | solution.py:9
  313.4 6.7 %subtract_select_fusion = f32[512,1024]{1,0:T(8,128)} fusion(f32[512,1024]{1,0:T(8,128)} %param.6, f32[512,512]{1,0:T(8,128)S(1)} %bitcast.11, f32[512,512]{1,0:T(8,128)} %get-tuple-element.2, f32[512,512]{1,0:T(8,128)} %get-tuple-element.3, pred[1024]{0:T(1024)(128)(4,1)S(1)} %fusion.8), kind=kOutput, calls=%fused_computation | convolution fusion | flops 3222798336 | bytes 7341056 | tf_op jit(solution)/shard_map/dot_general | solution.py:32
  (2 shorter events, 0.0 us)
Async XLA Ops:
  7.2 65.2 %copy-start = (f32[32,512]{1,0:T(8,128)S(1)}, f32[32,512]{1,0:T(8,128)}, u32[]{:S(2)}) copy-start(f32[32,512]{1,0:T(8,128)} %param.7) | copy-start | bytes 196612
  7.2 65.1 %all-gather.2.cloned.1.call-start = ((), (), s32[]{:S(2)}) async-start(), calls=%async_computation.1 | async-start | bytes 1114112 | tf_op jit(solution)/shard_map/all_gather | solution.py:15
  75.4 18.7 %all-to-all-start = ((f32[16,32,512]{2,1,0:T(8,128)}), f32[16,32,512]{2,1,0:T(8,128)S(1)}, u32[]{:S(2)}, u32[]{:S(2)}) async-start(f32[16,32,512]{2,1,0:T(8,128)} %stack.2), calls=%async_computation | async-start | bytes 2097152 | tf_op jit(solution)/shard_map/all_to_all | solution.py:20
  79.7 233.7 %all-reduce.3.cloned.1.call-start = ((), (), s32[]{:S(2)}) async-start(), calls=%async_computation.2 | async-start | bytes 4194304 | tf_op jit(solution)/shard_map/psum | solution.py:9
  79.8 15.8 %copy-start.3 = (f32[16,64]{1,0:T(8,128)S(1)}, f32[16,64]{1,0:T(8,128)}, u32[]{:S(2)}) copy-start(f32[16,64]{1,0:T(8,128)} %param.10) | copy-start | bytes 12292
  79.8 51.3 %copy-start.4 = (s32[64]{0:T(128)S(1)}, s32[64]{0:T(128)}, u32[]{:S(2)}) copy-start(s32[64]{0:T(128)} %param.11) | copy-start | bytes 772
  79.8 51.4 %copy-start.1 = (f32[512,512]{0,1:T(8,128)S(1)}, f32[512,512]{0,1:T(8,128)}, u32[]{:S(2)}) copy-start(f32[512,512]{0,1:T(8,128)} %all-gather.2.cloned.1.call-done) | copy-start | bytes 3145732
  95.6 37.4 %copy-start.2 = (f32[512,64]{0,1:T(8,128)S(1)}, f32[512,64]{0,1:T(8,128)}, u32[]{:S(2)}) copy-start(f32[512,64]{0,1:T(8,128)} %param.9) | copy-start | bytes 393220
Sparse Core Ops, SparseCore 0:
  11.0 61.2 all-gather.1
  95.7 217.6 all-reduce.2
